TPU v7x, 512 devices: a whole 4x8x8 slice. The times are simulated.
512 devices in a mesh: row: 32 (over y, x), col: 16 (over z, core).
Axes of the slice: x: 4, y: 8, z: 8, core: 2. Of those that a mesh axis runs over, the one named last changes fastest.
Arguments:
- kernel_matrix: float32 [16384, 16384], P('row', 'col'), may hold values from 0 to 2, as said below
Outputs:
- factored: float32 [16384, 16384], P('row', 'col')
Inputs may be any that keep to these rules, and one draw needn't show every extreme that they name: kernel_matrix, put in global order by the element-cyclic map, is symmetric: a Gaussian-process kernel amp * exp(-distance / scale) over random points plus a nugget of at least 0.5 on the diagonal, so it is positive definite with smallest eigenvalue at least 0.5.
All inputs are finite; a program needn't handle non-finite values.
Results may differ from a plain program's by a relative error of at most 0.00025.
Values sent between devices are 32-bit elements; how exact they have to be, the bound alone decides.
No kernel may reach another device: no remote copies, remote signals or barrier semaphores. Data moves between devices by JAX's collectives and lax.ppermute only.
A program may use at most 64 MiB of HBM per device.

v0:
```python
import jax
import jax.numpy as jnp
from jax import lax
from jax.sharding import PartitionSpec as P

PANEL = 192
PANELS = 2


def spread(block, axis, source):
    block = jnp.where(lax.axis_index(axis) == source, block, jnp.zeros_like(block))
    return lax.psum(block, axis)


def solve_rows(lower_factor, rows):
    return lax.linalg.triangular_solve(
        lower_factor, rows, left_side=False, lower=True, transpose_a=True
    )


def alternate_cols(block, groups):
    height = block.shape[0]
    inner = block.shape[1] // groups
    return block.reshape(height, groups, inner).transpose(0, 2, 1).reshape(height, groups * inner)


def alternate_rows(block, groups):
    inner = block.shape[0] // groups
    breadth = block.shape[1]
    return block.reshape(groups, inner, breadth).transpose(1, 0, 2).reshape(groups * inner, breadth)


def per_device(kernel_matrix):
    matrix = kernel_matrix
    row_count = lax.axis_size("row")
    col_count = lax.axis_size("col")
    row_share = row_count // col_count
    local_rows, local_cols = matrix.shape
    tile_rows = PANEL // row_count
    tile_cols = PANEL // col_count
    col_index = lax.axis_index("col")
    for current in range(PANELS):
        factor_row_start = current * tile_rows
        factor_col_start = current * tile_cols
        factor_col_rest = factor_col_start + tile_cols
        corner = matrix[
            factor_row_start : factor_row_start + tile_rows, factor_col_start:factor_col_rest
        ]
        corner = lax.all_gather(corner, "row", axis=0, tiled=True)
        corner = lax.all_gather(corner, "col", axis=1, tiled=True)
        corner = alternate_cols(alternate_rows(corner, row_count), col_count)
        lower_factor = jnp.linalg.cholesky(corner)
        column_block = matrix[:, factor_col_start:factor_col_rest]
        gathered = alternate_cols(
            lax.all_gather(column_block, "col", axis=1, tiled=True), col_count
        )
        factor_left_rows = solve_rows(lower_factor, gathered)
        received = []
        for source in range(row_share):
            received.append(spread(factor_left_rows, "row", col_index + source * col_count))
        factor_right_rows = jnp.stack(received, axis=1).reshape(local_cols, PANEL)[factor_col_rest:]
        row_start = current * tile_rows
        col_start = current * tile_cols
        owned = factor_left_rows.reshape(local_rows, tile_cols, col_count)
        owned = lax.dynamic_index_in_dim(owned, col_index, axis=2, keepdims=False)
        matrix = matrix.at[row_start:, col_start : col_start + tile_cols].set(owned[row_start:])
        row_low = (current + 1) * tile_rows
        col_low = (current + 1) * tile_cols
        term = jnp.dot(
            factor_left_rows[row_low:local_rows],
            factor_right_rows.T,
            precision=lax.Precision.HIGHEST,
            preferred_element_type=jnp.float32,
        )
        matrix = matrix.at[row_low:local_rows, col_low:local_cols].add(-term)
    return matrix


def solution(mesh):
    in_specs = (P("row", "col"),)
    out_specs = P("row", "col")
    return jax.shard_map(
        per_device, mesh=mesh, in_specs=in_specs, out_specs=out_specs, check_vma=False
    )
```

profile of v0, /device:TPU:16, one launch (start us, length us, event | category | flops | bytes accessed | tf_op | source)
XLA Modules:
  0.0 630.4 jit_solution(13229825803608452660)
XLA Ops:
  6.5 1.9 copy.35
  9.2 24.6 %all-gather.2 = f32[16,12,512]{2,1,0:T(8,128)S(1)} all-gather(f32[1,12,512]{2,1,0:T(8,128)S(1)} %slice_bitcast_fusion.11), channel_id=1, replica_groups=mesh['row'=32,'col'=16] {'col'}, dimensions={0}, use_global_device_ids=true | all-gather | bytes 417792 | tf_op jit(solution)/shard_map/all_gather | solution.py:55
  34.1 39.3 %all-gather = f32[32,6,12]{2,1,0:T(8,128)S(1)} all-gather(f32[1,6,12]{2,1,0:T(8,128)S(1)} %slice_bitcast_fusion.12), channel_id=1, replica_groups=mesh['row'=32,'col'=16] {'row'}, dimensions={0}, use_global_device_ids=true | all-gather | bytes 9504 | tf_op jit(solution)/shard_map/all_gather | solution.py:49
  73.5 14.9 %all-gather.1 = f32[16,12,192]{2,1,0:T(8,128)S(1)} all-gather(f32[1,12,192]{2,1,0:T(8,128)S(1)} %bitcast.133), channel_id=1, replica_groups=mesh['row'=32,'col'=16] {'col'}, dimensions={0}, use_global_device_ids=true | all-gather | bytes 156672 | tf_op jit(solution)/shard_map/all_gather | solution.py:50
  89.4 11.7 %cholesky.136 = f32[128,128]{1,0:T(8,128)S(1)} custom-call(f32[128,128]{1,0:T(8,128)S(1)} %cholesky.208), custom_call_target="Cholesky" | custom-call | tf_op jit(solution)/shard_map/jit(cholesky)/cholesky | solution.py:52
  101.1 9.8 %custom-call.13 = f32[1,128,128]{1,2,0:T(8,128)S(1)} custom-call(f32[1,128,128]{2,1,0:T(8,128)S(1)} %get-tuple-element.94), custom_call_target="InvertDiagBlocksLowerTriangular" | custom-call | tf_op jit(solution)/shard_map/jit(cholesky)/cholesky | solution.py:52
  111.3 5.8 cholesky.156
  120.7 19.7 %custom-call.14 = f32[2,128,128]{1,2,0:T(8,128)S(1)} custom-call(f32[2,128,128]{2,1,0:T(8,128)S(1)} %pad_maximum_fusion.4), custom_call_target="InvertDiagBlocksLowerTriangular" | custom-call | tf_op jit(solution)/shard_map/triangular_solve/custom-call.0 | solution.py:16
  141.8 1.1 fusion.19
  145.7 153.4 %all-reduce.10.cloned.1.call-done = (f32[512,1,192]{0,2,1:T(8,128)}, f32[512,1,192]{0,2,1:T(8,128)}) async-done(((f32[512,1,192]{0,2,1:T(8,128)}, f32[512,1,192]{0,2,1:T(8,128)}), (f32[512,1,192]{0,2,1:T(8,128)}, f32[512,1,192]{0,2,1:T(8,128)})) %all-reduce.10.cloned.1.call-update) | async-done | bytes 786448 | tf_op jit(solution)/shard_map/psum | solution.py:12
  299.1 1.4 pad_maximum_fusion.1
  300.5 1.3 copy.36
  301.8 1.9 slice.169
  303.8 2.1 slice_add_fusion
  305.8 1.3 copy-done
  307.2 36.3 %all-gather.3 = f32[32,6,12]{2,1,0:T(8,128)S(1)} all-gather(f32[1,6,12]{2,1,0:T(8,128)S(1)} %bitcast.135), channel_id=1, replica_groups=mesh['row'=32,'col'=16] {'row'}, dimensions={0}, use_global_device_ids=true | all-gather | bytes 9504 | tf_op jit(solution)/shard_map/all_gather | solution.py:49
  343.6 18.8 %all-gather.4 = f32[16,12,192]{2,1,0:T(8,128)S(1)} all-gather(f32[1,12,192]{2,1,0:T(8,128)S(1)} %bitcast.134), channel_id=1, replica_groups=mesh['row'=32,'col'=16] {'col'}, dimensions={0}, use_global_device_ids=true | all-gather | bytes 156672 | tf_op jit(solution)/shard_map/all_gather | solution.py:50
  363.4 11.7 %cholesky.174 = f32[128,128]{1,0:T(8,128)S(1)} custom-call(f32[128,128]{1,0:T(8,128)S(1)} %cholesky.211), custom_call_target="Cholesky" | custom-call | tf_op jit(solution)/shard_map/jit(cholesky)/cholesky | solution.py:52
  375.2 9.8 %custom-call.15 = f32[1,128,128]{1,2,0:T(8,128)S(1)} custom-call(f32[1,128,128]{2,1,0:T(8,128)S(1)} %get-tuple-element.92), custom_call_target="InvertDiagBlocksLowerTriangular" | custom-call | tf_op jit(solution)/shard_map/jit(cholesky)/cholesky | solution.py:52
  385.4 5.8 cholesky.194
  394.0 10.9 %scatter-add.6 = f32[512,1024]{0,1:T(8,128)S(1)} dynamic-update-slice(f32[512,1024]{0,1:T(8,128)S(1)} %scatter.6, f32[506,1012]{0,1:T(8,128)} %copy-done, s32[]{:T(128)} %constant.182.clone.1, s32[]{:T(128)} %constant.183.clone.1) | dynamic-update-slice | bytes 4096580 | tf_op jit(solution)/shard_map/scatter-add | solution.py:75
  404.9 16.4 %all-gather.5 = f32[16,12,512]{2,1,0:T(8,128)S(1)} all-gather(f32[1,12,512]{2,1,0:T(8,128)S(1)} %slice_bitcast_fusion.8), channel_id=1, replica_groups=mesh['row'=32,'col'=16] {'col'}, dimensions={0}, use_global_device_ids=true | all-gather | bytes 417792 | tf_op jit(solution)/shard_map/all_gather | solution.py:55
  421.7 19.7 %custom-call.16 = f32[2,128,128]{1,2,0:T(8,128)S(1)} custom-call(f32[2,128,128]{2,1,0:T(8,128)S(1)} %pad_maximum_fusion.5), custom_call_target="InvertDiagBlocksLowerTriangular" | custom-call | tf_op jit(solution)/shard_map/triangular_solve/custom-call.0 | solution.py:16
  442.4 1.0 select_bitcast_fusion.1
  443.6 1.1 scatter.9
  444.7 155.9 %all-reduce.8.cloned.1.call-done = (f32[512,1,192]{0,2,1:T(8,128)}, f32[512,1,192]{0,2,1:T(8,128)}) async-done(((f32[512,1,192]{0,2,1:T(8,128)}, f32[512,1,192]{0,2,1:T(8,128)}), (f32[512,1,192]{0,2,1:T(8,128)}, f32[512,1,192]{0,2,1:T(8,128)})) %all-reduce.8.cloned.1.call-update) | async-done | bytes 786448 | tf_op jit(solution)/shard_map/psum | solution.py:12
  600.6 2.3 pad_maximum_fusion
  602.9 1.9 copy.45
  604.8 1.7 slice.176
  606.5 4.5 slice_add_fusion.1
  611.0 10.8 %scatter-add.9 = f32[512,1024]{0,1:T(8,128)S(1)} dynamic-update-slice(f32[512,1024]{0,1:T(8,128)S(1)} %scatter.9, f32[500,1000]{0,1:T(8,128)} %slice_add_fusion.1, s32[]{:T(128)} %constant.183.clone.1, s32[]{:T(128)} %constant.184.clone.1) | dynamic-update-slice | bytes 4000004 | tf_op jit(solution)/shard_map/scatter-add | solution.py:75
  621.8 1.8 copy.46
  (81 shorter events, 13.4 us)
Async XLA Ops:
  6.5 292.6 %all-reduce.10.cloned.1.call-start = ((), (), s32[]{:S(2)}) async-start(), calls=%async_computation.1 | async-start | bytes 1572864 | tf_op jit(solution)/shard_map/psum | solution.py:12
  120.0 0.6 copy-start.1
  140.4 0.7 copy-start.3
  143.9 456.7 %all-reduce.8.cloned.1.call-start = ((), (), s32[]{:S(2)}) async-start(), calls=%async_computation | async-start | bytes 1572864 | tf_op jit(solution)/shard_map/psum | solution.py:12
  305.8 1.3 copy-start
  404.8 16.7 %copy-start.2 = (f32[128,64]{1,0:T(8,128)S(1)}, f32[128,64]{1,0:T(8,128)}, u32[]{:S(2)}) copy-start(f32[128,64]{1,0:T(8,128)} %copy-done.1) | copy-start | bytes 98308
Sparse Core Ops, SparseCore 0:
  144.0 155.0 all-reduce.9
  443.6 156.9 all-reduce.7
where the time goes:
time: 631 us; the launch traced here: 630 us
  waiting for transfers between devices  309 us (49%)
  blocking collectives  150 us (24%)
  other arithmetic  104 us (16%)
  local copies, waits for them, and re-layouts  39.9 us (6%)
  between operations  16.5 us (3%)
  matrix products  10.2 us (2%)
    psum x2, waiting for transfers between devices, spread(): return lax.psum(block, axis)  309 us
    all_gather x2, blocking collectives, per_device(): corner = lax.all_gather(corner, 'row', axis=0, tiled=True)  75.6 us
    another operation x14, other arithmetic, per_device(): lower_factor = jnp.linalg.cholesky(corner)  57.6 us
    all_gather x2, blocking collectives, per_device(): lax.all_gather(column_block, 'col', axis=1, tiled=True)  41 us
    another operation x10, other arithmetic, solve_rows(): lax.linalg.triangular_solve(lower_factor, rows, left_side=False, lower=Tr...  39.6 us
    all_gather x2, blocking collectives, per_device(): corner = lax.all_gather(corner, 'col', axis=1, tiled=True)  33.6 us
    scatter-add x3, local copies, waits for them, and re-layouts, per_device(): matrix = matrix.at[row_low:local_rows, col_low:local_cols].add(-term)  23.4 us
  transfers between devices with their start and end apart: 2, of which 2 were waited for; matrix products, arithmetic and copies ran while one was open for 0% of the time, Pallas kernels for 0%

commit v1 on v0

--- a/solution.py
+++ b/solution.py
@@ -9,7 +9,7 @@
 
 def spread(block, axis, source):
     block = jnp.where(lax.axis_index(axis) == source, block, jnp.zeros_like(block))
-    return lax.psum(block, axis)
+    return jnp.sum(lax.all_gather(block, axis), axis=0)
 
 
 def solve_rows(lower_factor, rows):

time: 631 us -> 868 us (1.38)
  the two profiles are of different devices: /device:TPU:16 before, /device:TPU:1 now
where the time goes in v1:
time: 868 us; the launch traced here: 857 us
  waiting for transfers between devices  427 us (49%)
  blocking collectives  154 us (18%)
  other arithmetic  131 us (15%)
  local copies, waits for them, and re-layouts  119 us (14%)
  between operations  16.8 us (2%)
  matrix products  9.37 us (1%)
    all_gather x4, waiting for transfers between devices, spread(): return jnp.sum(lax.all_gather(block, axis), axis=0)  426 us
    unnamed x29, local copies, waits for them, and re-layouts  84.5 us
    all_gather x2, blocking collectives, per_device(): corner = lax.all_gather(corner, 'row', axis=0, tiled=True)  60.6 us
    another operation x14, other arithmetic, per_device(): lower_factor = jnp.linalg.cholesky(corner)  57.6 us
    all_gather x2, blocking collectives, per_device(): corner = lax.all_gather(corner, 'col', axis=1, tiled=True)  51.6 us
    all_gather x2, blocking collectives, per_device(): lax.all_gather(column_block, 'col', axis=1, tiled=True)  42.1 us
    another operation x10, other arithmetic, solve_rows(): lax.linalg.triangular_solve(lower_factor, rows, left_side=False, lower=Tr...  39.6 us
    reduce_sum x4, other arithmetic, spread(): return jnp.sum(lax.all_gather(block, axis), axis=0)  28.9 us
  transfers between devices with their start and end apart: 4, of which 4 were waited for; matrix products, arithmetic and copies ran while one was open for 7% of the time, Pallas kernels for 0%

profile of v1, /device:TPU:1, one launch (start us, length us, event | category | flops | bytes accessed | tf_op | source)
XLA Modules:
  0.0 857.5 jit_solution(1476597996959150635)
XLA Ops:
  6.5 1.9 copy.52
  9.2 25.9 %all-gather.6 = f32[16,12,512]{2,1,0:T(8,128)S(1)} all-gather(f32[1,12,512]{2,1,0:T(8,128)S(1)} %slice_bitcast_fusion.11), channel_id=1, replica_groups=mesh['row'=32,'col'=16] {'col'}, dimensions={0}, use_global_device_ids=true | all-gather | bytes 417792 | tf_op jit(solution)/shard_map/all_gather | solution.py:55
  35.4 31.9 %all-gather.4 = f32[32,6,12]{2,1,0:T(8,128)S(1)} all-gather(f32[1,6,12]{2,1,0:T(8,128)S(1)} %slice_bitcast_fusion.12), channel_id=1, replica_groups=mesh['row'=32,'col'=16] {'row'}, dimensions={0}, use_global_device_ids=true | all-gather | bytes 9504 | tf_op jit(solution)/shard_map/all_gather | solution.py:49
  67.4 23.0 %all-gather.5 = f32[16,12,192]{2,1,0:T(8,128)S(1)} all-gather(f32[1,12,192]{2,1,0:T(8,128)S(1)} %bitcast.157), channel_id=1, replica_groups=mesh['row'=32,'col'=16] {'col'}, dimensions={0}, use_global_device_ids=true | all-gather | bytes 156672 | tf_op jit(solution)/shard_map/all_gather | solution.py:50
  91.4 11.7 %cholesky.136 = f32[128,128]{1,0:T(8,128)S(1)} custom-call(f32[128,128]{1,0:T(8,128)S(1)} %cholesky.208), custom_call_target="Cholesky" | custom-call | tf_op jit(solution)/shard_map/jit(cholesky)/cholesky | solution.py:52
  103.2 9.8 %custom-call.13 = f32[1,128,128]{1,2,0:T(8,128)S(1)} custom-call(f32[1,128,128]{2,1,0:T(8,128)S(1)} %get-tuple-element.90), custom_call_target="InvertDiagBlocksLowerTriangular" | custom-call | tf_op jit(solution)/shard_map/jit(cholesky)/cholesky | solution.py:52
  113.4 5.8 cholesky.156
  122.1 19.7 %custom-call.14 = f32[2,128,128]{1,2,0:T(8,128)S(1)} custom-call(f32[2,128,128]{2,1,0:T(8,128)S(1)} %pad_maximum_fusion.4), custom_call_target="InvertDiagBlocksLowerTriangular" | custom-call | tf_op jit(solution)/shard_map/triangular_solve/custom-call.0 | solution.py:16
  146.7 114.4 %all-gather.17.cloned.1.call-done = f32[16384,192]{0,1:T(8,128)} async-done(((f32[512,192]{0,1:T(8,128)}), f32[16384,192]{0,1:T(8,128)}) %all-gather.17.cloned.1.call-update) | async-done | bytes 12582928 | tf_op jit(solution)/shard_map/all_gather | solution.py:12
  261.1 20.0 %copy.70 = f32[24,8,32,512]{3,2,1,0:T(8,128)} copy(f32[24,8,32,512]{3,1,2,0:T(8,128)} %bitcast.126) | data formatting | bytes 25165824
  281.0 7.4 bitcast_reduce_fusion.2
  288.4 97.3 %all-gather.15.cloned.1.call-done = f32[16384,192]{0,1:T(8,128)} async-done(((f32[512,192]{0,1:T(8,128)}), f32[16384,192]{0,1:T(8,128)}) %all-gather.15.cloned.1.call-update) | async-done | bytes 12582928 | tf_op jit(solution)/shard_map/all_gather | solution.py:12
  385.7 20.1 %copy.69 = f32[24,8,32,512]{3,2,1,0:T(8,128)} copy(f32[24,8,32,512]{3,1,2,0:T(8,128)} %bitcast.127) | data formatting | bytes 25165824
  405.7 7.1 bitcast_reduce_fusion.3
  414.4 1.9 slice.169
  416.3 2.1 slice_add_fusion
  419.8 28.8 %all-gather.7 = f32[32,6,12]{2,1,0:T(8,128)S(1)} all-gather(f32[1,6,12]{2,1,0:T(8,128)S(1)} %bitcast.159), channel_id=1, replica_groups=mesh['row'=32,'col'=16] {'row'}, dimensions={0}, use_global_device_ids=true | all-gather | bytes 9504 | tf_op jit(solution)/shard_map/all_gather | solution.py:49
  448.6 28.6 %all-gather.8 = f32[16,12,192]{2,1,0:T(8,128)S(1)} all-gather(f32[1,12,192]{2,1,0:T(8,128)S(1)} %bitcast.158), channel_id=1, replica_groups=mesh['row'=32,'col'=16] {'col'}, dimensions={0}, use_global_device_ids=true | all-gather | bytes 156672 | tf_op jit(solution)/shard_map/all_gather | solution.py:50
  478.3 11.7 %cholesky.174 = f32[128,128]{1,0:T(8,128)S(1)} custom-call(f32[128,128]{1,0:T(8,128)S(1)} %cholesky.211), custom_call_target="Cholesky" | custom-call | tf_op jit(solution)/shard_map/jit(cholesky)/cholesky | solution.py:52
  490.1 9.8 %custom-call.15 = f32[1,128,128]{1,2,0:T(8,128)S(1)} custom-call(f32[1,128,128]{2,1,0:T(8,128)S(1)} %get-tuple-element.88), custom_call_target="InvertDiagBlocksLowerTriangular" | custom-call | tf_op jit(solution)/shard_map/jit(cholesky)/cholesky | solution.py:52
  500.3 5.8 cholesky.194
  508.8 10.9 %scatter-add.6 = f32[512,1024]{0,1:T(8,128)S(1)} dynamic-update-slice(f32[512,1024]{0,1:T(8,128)S(1)} %scatter.6, f32[506,1012]{0,1:T(8,128)} %copy-done, s32[]{:T(128)} %constant.183.clone.1, s32[]{:T(128)} %constant.184.clone.1) | dynamic-update-slice | bytes 4096580 | tf_op jit(solution)/shard_map/scatter-add | solution.py:75
  519.7 16.2 %all-gather.9 = f32[16,12,512]{2,1,0:T(8,128)S(1)} all-gather(f32[1,12,512]{2,1,0:T(8,128)S(1)} %slice_bitcast_fusion.8), channel_id=1, replica_groups=mesh['row'=32,'col'=16] {'col'}, dimensions={0}, use_global_device_ids=true | all-gather | bytes 417792 | tf_op jit(solution)/shard_map/all_gather | solution.py:55
  536.3 19.7 %custom-call.16 = f32[2,128,128]{1,2,0:T(8,128)S(1)} custom-call(f32[2,128,128]{2,1,0:T(8,128)S(1)} %pad_maximum_fusion.5), custom_call_target="InvertDiagBlocksLowerTriangular" | custom-call | tf_op jit(solution)/shard_map/triangular_solve/custom-call.0 | solution.py:16
  560.1 117.0 %all-gather.21.cloned.1.call-done = f32[16384,192]{0,1:T(8,128)} async-done(((f32[512,192]{0,1:T(8,128)}), f32[16384,192]{0,1:T(8,128)}) %all-gather.21.cloned.1.call-update) | async-done | bytes 12582928 | tf_op jit(solution)/shard_map/all_gather | solution.py:12
  677.1 20.0 %copy.72 = f32[24,8,32,512]{3,2,1,0:T(8,128)} copy(f32[24,8,32,512]{3,1,2,0:T(8,128)} %bitcast.128) | data formatting | bytes 25165824
  697.0 7.4 bitcast_reduce_fusion
  704.5 97.1 %all-gather.19.cloned.1.call-done = f32[16384,192]{0,1:T(8,128)} async-done(((f32[512,192]{0,1:T(8,128)}), f32[16384,192]{0,1:T(8,128)}) %all-gather.19.cloned.1.call-update) | async-done | bytes 12582928 | tf_op jit(solution)/shard_map/all_gather | solution.py:12
  801.5 20.1 %copy.71 = f32[24,8,32,512]{3,2,1,0:T(8,128)} copy(f32[24,8,32,512]{3,1,2,0:T(8,128)} %bitcast.129) | data formatting | bytes 25165824
  821.6 7.1 bitcast_reduce_fusion.1
  833.4 4.5 slice_add_fusion.1
  837.9 10.8 %scatter-add.9 = f32[512,1024]{0,1:T(8,128)S(1)} dynamic-update-slice(f32[512,1024]{0,1:T(8,128)S(1)} %scatter.9, f32[500,1000]{0,1:T(8,128)} %slice_add_fusion.1, s32[]{:T(128)} %constant.184.clone.1, s32[]{:T(128)} %constant.185.clone.1) | dynamic-update-slice | bytes 4000004 | tf_op jit(solution)/shard_map/scatter-add | solution.py:75
  (97 shorter events, 25.7 us)
Async XLA Ops:
  6.5 254.6 %all-gather.17.cloned.1.call-start = ((), (), s32[]{:S(2)}) async-start(), calls=%async_computation.1 | async-start | bytes 12976128 | tf_op jit(solution)/shard_map/all_gather | solution.py:12
  122.0 19.8 %copy-start.3 = (f32[128,64]{1,0:T(8,128)}, f32[128,64]{1,0:T(8,128)S(1)}, u32[]{:S(2)}) copy-start(f32[128,64]{1,0:T(8,128)S(1)} %pad_convert_fusion) | copy-start | bytes 98308
  142.9 138.2 %copy-start.1 = (f32[512,64]{0,1:T(8,128)}, f32[512,64]{0,1:T(8,128)S(1)}, u32[]{:S(2)}) copy-start(f32[512,64]{0,1:T(8,128)S(1)} %fusion.19) | copy-start | bytes 393220
  144.0 241.7 %all-gather.15.cloned.1.call-start = ((), (), s32[]{:S(2)}) async-start(), calls=%async_computation | async-start | bytes 12976128 | tf_op jit(solution)/shard_map/all_gather | solution.py:12
  144.7 532.4 %all-gather.21.cloned.1.call-start = ((), (), s32[]{:S(2)}) async-start(), calls=%async_computation.3 | async-start | bytes 12976128 | tf_op jit(solution)/shard_map/all_gather | solution.py:12
  413.0 3.3 copy-start.2
  418.4 1.3 copy-start
  519.7 16.5 %copy-start.4 = (f32[128,64]{1,0:T(8,128)S(1)}, f32[128,64]{1,0:T(8,128)}, u32[]{:S(2)}) copy-start(f32[128,64]{1,0:T(8,128)} %copy-done.3) | copy-start | bytes 98308
  558.1 243.4 %all-gather.19.cloned.1.call-start = ((), (), s32[]{:S(2)}) async-start(), calls=%async_computation.2 | async-start | bytes 12976128 | tf_op jit(solution)/shard_map/all_gather | solution.py:12
Sparse Core Ops, SparseCore 0:
  144.1 116.9 all-gather.16
  264.3 121.3 all-gather.14
  558.3 118.7 all-gather.20
  680.1 121.3 all-gather.18
